TPU v7x, 32 devices: a whole 2x2x4 slice. The times are simulated.
32 devices in a mesh: groups: 2 (over y), replica: 1, da: 4 (over x, core), db: 4 (over z).
Axes of the slice: x: 2, y: 2, z: 4, core: 2. Of those that a mesh axis runs over, the one named last changes fastest.
Arguments:
- tokens: bfloat16 [4096, 1024], P(('groups', 'replica', 'da', 'db')), parts along dimension 0, may hold values from -6 to 6
- grad_out: bfloat16 [4096, 1024], P(('groups', 'replica', 'da', 'db')), parts along dimension 0, may hold values from -3 to 3
- routes: int32 [4096, 8], P(('groups', 'replica', 'da', 'db')), parts along dimension 0, may hold values from 0 to 15, as said below
- gates: bfloat16 [4096, 8], P(('groups', 'replica', 'da', 'db')), parts along dimension 0, may hold values from 0.019897461 to 0.5
- w_gate_up: bfloat16 [16, 1024, 768], P(('da', 'db'), 'replica'), may hold values from -0.1875 to 0.1875
- w_down: bfloat16 [16, 384, 1024], P(('da', 'db'), 'replica'), may hold values from -0.3125 to 0.3125
Outputs:
- token_grads: bfloat16 [4096, 1024], P(('groups', 'replica', 'da', 'db')), parts along dimension 0
- gate_grads: bfloat16 [4096, 8], P(('groups', 'replica', 'da', 'db')), parts along dimension 0
- gate_up_grads: bfloat16 [32, 1024, 768], P(('groups', 'da', 'db'), 'replica'), parts along dimension 0
- down_grads: bfloat16 [32, 384, 1024], P(('groups', 'da', 'db'), 'replica'), parts along dimension 0
There are 2 independent parts, one for each index of `groups`. A program takes and returns all parts, laid end to end along the dimension named above; an argument that names none is the same for every part. Nothing has to cross between parts.
Inputs may be any that keep to these rules, and one draw needn't show every extreme that they name: `routes`: each token names 8 different experts. In every aligned block of 2 consecutive tokens, each expert is named exactly once, so the tokens of one device name every expert exactly 64 times.
All inputs are finite; a program needn't handle non-finite values.
Results may differ from a plain program's by a relative error of at most 0.0085.
Values may be sent and summed in bfloat16 or wider, within the bound.
A program may use at most 64 MiB of HBM per device.

v0:
```python
import jax
import jax.numpy as jnp
from jax import lax
from jax.sharding import PartitionSpec as P


def silu_parts(projected):
    sigmoid = jax.nn.sigmoid(projected)
    return (projected * sigmoid, sigmoid * (1.0 + projected * (1.0 - sigmoid)))


def body(tokens, grad_out, routes, gates, w_gate_up, w_down):
    local_tokens, features = tokens.shape
    top_count = routes.shape[1]
    hidden_units = w_gate_up.shape[2] // 2
    first_size = lax.axis_size("da")
    second_size = lax.axis_size("db")
    experts = first_size * second_size
    per_round = experts // top_count
    rounds = local_tokens // per_round
    expert_ids = lax.broadcasted_iota(jnp.int32, (1, 1, 1, experts), 3)
    matches = routes.reshape(rounds, per_round, top_count, 1) == expert_ids
    gate_values = gates.reshape(rounds, per_round, top_count, 1).astype(jnp.float32)
    gate_table = jnp.sum(jnp.where(matches, gate_values, 0.0), axis=(1, 2)).astype(jnp.bfloat16)
    chosen = jnp.any(matches, axis=2).astype(jnp.bfloat16)
    input_send = jnp.einsum(
        "rge,rgd->red",
        chosen,
        tokens.reshape(rounds, per_round, features),
        preferred_element_type=jnp.float32,
    ).astype(jnp.bfloat16)
    upstream_send = jnp.einsum(
        "rge,rgd->red",
        chosen,
        grad_out.reshape(rounds, per_round, features),
        preferred_element_type=jnp.float32,
    ).astype(jnp.bfloat16)
    input_recv, upstream_recv, gate_recv = (
        lax.all_to_all(input_send, ("da", "db"), split_axis=1, concat_axis=1, tiled=True),
        lax.all_to_all(upstream_send, ("da", "db"), split_axis=1, concat_axis=1, tiled=True),
        lax.all_to_all(gate_table, ("da", "db"), split_axis=1, concat_axis=1, tiled=True),
    )
    input_rows = input_recv.reshape(-1, features)
    upstream_rows = upstream_recv.reshape(-1, features)
    gate_rows = gate_recv.reshape(-1, 1).astype(jnp.float32)
    w_in, w_out = (
        lax.all_gather(w_gate_up[0], "replica", axis=0, tiled=True),
        lax.all_gather(w_down[0], "replica", axis=0, tiled=True),
    )
    projected = jnp.dot(input_rows, w_in, preferred_element_type=jnp.float32)
    back_raw = jnp.einsum("rd,fd->rf", upstream_rows, w_out, preferred_element_type=jnp.float32)
    gate_part = projected[:, :hidden_units]
    up_part = projected[:, hidden_units:]
    activated, derivative = silu_parts(gate_part)
    hidden = (activated * up_part).astype(jnp.bfloat16)
    gate_scores = jnp.sum(hidden.astype(jnp.float32) * back_raw, axis=1).astype(jnp.bfloat16)
    back_hidden = gate_rows * back_raw
    grad_projected = jnp.concatenate(
        [back_hidden * up_part * derivative, back_hidden * activated], axis=1
    ).astype(jnp.bfloat16)
    scaled_upstream = (gate_rows * upstream_rows.astype(jnp.float32)).astype(jnp.bfloat16)
    input_grads = jnp.einsum("rf,df->rd", grad_projected, w_in, preferred_element_type=jnp.float32)
    input_grads = input_grads.astype(jnp.bfloat16).reshape(rounds, experts, features)
    score_back = gate_scores.reshape(rounds, experts)
    returned, score_ret = (
        lax.all_to_all(input_grads, ("da", "db"), split_axis=1, concat_axis=1, tiled=True),
        lax.all_to_all(score_back, ("da", "db"), split_axis=1, concat_axis=1, tiled=True),
    )
    score_ret = score_ret.reshape(rounds, 1, 1, experts).astype(jnp.float32)
    token_grads = (
        jnp.einsum("rge,red->rgd", chosen, returned, preferred_element_type=jnp.float32)
        .astype(jnp.bfloat16)
        .reshape(local_tokens, features)
    )
    gate_grads = (
        jnp.sum(jnp.where(matches, score_ret, 0.0), axis=3)
        .astype(jnp.bfloat16)
        .reshape(local_tokens, top_count)
    )
    columns = input_rows
    grad_in = lax.psum_scatter(
        jnp.einsum("rd,rf->df", columns, grad_projected, preferred_element_type=jnp.float32).astype(
            jnp.bfloat16
        ),
        "replica",
        scatter_dimension=0,
        tiled=True,
    )
    columns = hidden
    grad_down = lax.psum_scatter(
        jnp.einsum(
            "rf,rd->fd", columns, scaled_upstream, preferred_element_type=jnp.float32
        ).astype(jnp.bfloat16),
        "replica",
        scatter_dimension=0,
        tiled=True,
    )
    return (token_grads, gate_grads, grad_in[None], grad_down[None])


def solution(mesh):
    placed = (
        P(("groups", "replica", "da", "db"), None),
        P(("groups", "replica", "da", "db"), None),
        P(("groups", "replica", "da", "db"), None),
        P(("groups", "replica", "da", "db"), None),
        P(("da", "db"), "replica", None),
        P(("da", "db"), "replica", None),
    )
    return jax.shard_map(
        body,
        mesh=mesh,
        in_specs=placed,
        out_specs=(
            P(("groups", "replica", "da", "db"), None),
            P(("groups", "replica", "da", "db"), None),
            P(("groups", "da", "db"), "replica", None),
            P(("groups", "da", "db"), "replica", None),
        ),
        check_vma=False,
    )
```

profile of v0, /device:TPU:0, one launch (start us, length us, event | category | flops | bytes accessed | tf_op | source)
XLA Modules:
  0.0 206.5 jit_solution(12314356661567460310)
XLA Ops:
  0.6 0.9 copy.56
  1.8 1.1 reshape.88
  3.6 2.5 %copy.67 = bf16[64,16,1024]{2,0,1:T(8,128)(2,1)} copy(bf16[64,16,1024]{2,1,0:T(8,128)(2,1)S(1)} %convolution_convert_fusion) | data formatting | bytes 4194304 | tf_op jit(solution)/shard_map/convert_element_type | solution.py:31
  6.1 7.6 %all-to-all-start.2 = ((bf16[64,16,1024]{2,0,1:T(8,128)(2,1)}), bf16[64,16,1024]{2,0,1:T(8,128)(2,1)}, u32[]{:S(2)}, u32[]{:S(2)}) async-start(bf16[64,16,1024]{2,0,1:T(8,128)(2,1)} %copy.67), calls=%async_computation.2 | async-start | bytes 4194304 | tf_op jit(solution)/shard_map/all_to_all | solution.py:39
  14.6 2.5 %copy.64 = bf16[64,16,1024]{2,0,1:T(8,128)(2,1)} copy(bf16[64,16,1024]{2,1,0:T(8,128)(2,1)S(1)} %convolution_convert_fusion.1) | data formatting | bytes 4194304 | tf_op jit(solution)/shard_map/convert_element_type | solution.py:37
  17.1 45.9 %all-to-all-done.2 = bf16[64,16,1024]{2,0,1:T(8,128)(2,1)} async-done(((bf16[64,16,1024]{2,0,1:T(8,128)(2,1)}), bf16[64,16,1024]{2,0,1:T(8,128)(2,1)}, u32[]{:S(2)}, u32[]{:S(2)}) %all-to-all-start.2) | async-done | bytes 2097184 | tf_op jit(solution)/shard_map/all_to_all | solution.py:39
  63.0 4.4 %all-to-all-start.1 = ((bf16[64,16,1024]{2,0,1:T(8,128)(2,1)}), bf16[64,16,1024]{2,0,1:T(8,128)(2,1)}, u32[]{:S(2)}, u32[]{:S(2)}) async-start(bf16[64,16,1024]{2,0,1:T(8,128)(2,1)} %copy.64), calls=%async_computation.1 | async-start | bytes 4194304 | tf_op jit(solution)/shard_map/all_to_all | solution.py:40
  67.5 2.7 %copy.68 = bf16[64,16,1024]{2,1,0:T(8,128)(2,1)S(1)} copy(bf16[64,16,1024]{2,0,1:T(8,128)(2,1)} %all-to-all-done.2) | data formatting | bytes 4194304 | tf_op jit(solution)/shard_map/all_to_all | solution.py:39
  70.3 1.4 copy-done.2
  71.6 3.5 %fusion.5 = f32[1024,768]{0,1:T(8,128)} fusion(bf16[1024,1024]{1,0:T(8,128)(2,1)S(1)} %bitcast.35, bf16[1,1024,768]{2,1,0:T(8,128)(2,1)S(1)} %copy-done), kind=kOutput, calls=%fused_computation.11 | convolution fusion | flops 1610612736 | bytes 6815744 | tf_op jit(solution)/shard_map/dot_general | solution.py:50
  75.1 41.7 %all-to-all-done.1 = bf16[64,16,1024]{2,0,1:T(8,128)(2,1)} async-done(((bf16[64,16,1024]{2,0,1:T(8,128)(2,1)}), bf16[64,16,1024]{2,0,1:T(8,128)(2,1)}, u32[]{:S(2)}, u32[]{:S(2)}) %all-to-all-start.1) | async-done | bytes 2097184 | tf_op jit(solution)/shard_map/all_to_all | solution.py:40
  116.8 2.9 %copy.65 = bf16[64,16,1024]{2,1,0:T(8,128)(2,1)S(1)} copy(bf16[64,16,1024]{2,0,1:T(8,128)(2,1)} %all-to-all-done.1) | data formatting | bytes 4194304 | tf_op jit(solution)/shard_map/all_to_all | solution.py:40
  119.8 2.1 multiply_reduce_fusion
  122.6 3.5 %all-to-all-start.4 = ((bf16[64,16,1]{0,2,1:T(2,128)(2,1)}), bf16[64,16,1]{0,2,1:T(2,128)(2,1)S(1)}, u32[]{:S(2)}, u32[]{:S(2)}) async-start(bf16[64,16,1]{0,2,1:T(2,128)(2,1)} %copy.72), calls=%async_computation.4 | async-start | bytes 16384 | tf_op jit(solution)/shard_map/all_to_all | solution.py:67
  126.3 6.1 %all-to-all-done.4 = bf16[64,16,1]{0,2,1:T(2,128)(2,1)S(1)} async-done(((bf16[64,16,1]{0,2,1:T(2,128)(2,1)}), bf16[64,16,1]{0,2,1:T(2,128)(2,1)S(1)}, u32[]{:S(2)}, u32[]{:S(2)}) %all-to-all-start.4) | async-done | bytes 2080 | tf_op jit(solution)/shard_map/all_to_all | solution.py:67
  132.5 9.0 %all_to_all.27 = bf16[64,16,1]{0,2,1:T(2,128)(2,1)S(1)} all-to-all(bf16[64,16,1]{0,2,1:T(2,128)(2,1)S(1)} %copy.60), channel_id=1, replica_groups=mesh['groups'=2,'replica'=1,'da'=4,'db'=4] {'da','db'}, dimensions={1} | all-to-all | bytes 4096 | tf_op jit(solution)/shard_map/all_to_all | solution.py:41
  141.6 2.8 %multiply_convert_fusion.4 = (bf16[1024,384]{0,1:T(8,128)(2,1)S(1)}, bf16[1024,384]{0,1:T(8,128)(2,1)S(1)}) fusion(f32[1024,768]{0,1:T(8,128)} %fusion.5, f32[1024,384]{0,1:T(8,128)S(1)} %get-tuple-element.30, f32[1024]{0:T(1024)S(1)} %reshape.93), kind=kLoop, calls=%fused_computation.16 | loop fusion | flops 5505024 | bytes 6295552 | tf_op jit(solution)/shard_map/convert.3
  144.4 1.9 convolution_convert_fusion.2
  146.3 2.5 %copy.69 = bf16[64,16,1024]{2,0,1:T(8,128)(2,1)} copy(bf16[64,16,1024]{2,1,0:T(8,128)(2,1)S(1)} %bitcast.39) | data formatting | bytes 4194304 | tf_op jit(solution)/shard_map/reshape | solution.py:63
  148.8 4.6 %all-to-all-start.3 = ((bf16[64,16,1024]{2,0,1:T(8,128)(2,1)}), bf16[64,16,1024]{2,0,1:T(8,128)(2,1)}, u32[]{:S(2)}, u32[]{:S(2)}) async-start(bf16[64,16,1024]{2,0,1:T(8,128)(2,1)} %copy.69), calls=%async_computation.3 | async-start | bytes 4194304 | tf_op jit(solution)/shard_map/all_to_all | solution.py:66
  154.2 3.7 %fusion.10 = bf16[1,384,1024]{2,1,0:T(8,128)(2,1)} fusion(bf16[1024,384]{0,1:T(8,128)(2,1)S(1)} %copy-done.12, bf16[1024,1024]{1,0:T(8,128)(2,1)} %bitcast.38, f32[1024]{0:T(1024)S(1)} %reshape.93), kind=kOutput, calls=%fused_computation.21 | convolution fusion | flops 808845312 | bytes 3674112 | tf_op jit(solution)/shard_map/rf,rd->fd/dot_general | solution.py:91
  157.9 3.0 %fusion.8 = bf16[1,1024,768]{2,1,0:T(8,128)(2,1)} fusion(bf16[1024,1024]{1,0:T(8,128)(2,1)S(1)} %bitcast.36, bf16[1024,384]{0,1:T(8,128)(2,1)S(1)} %copy-done.8, bf16[1024,384]{0,1:T(8,128)(2,1)S(1)} %copy-done.6), kind=kOutput, calls=%fused_computation.19 | convolution fusion | flops 1614544896 | bytes 5242880 | tf_op jit(solution)/shard_map/rd,rf->df/dot_general | solution.py:82
  160.9 41.9 %all-to-all-done.3 = bf16[64,16,1024]{2,0,1:T(8,128)(2,1)} async-done(((bf16[64,16,1024]{2,0,1:T(8,128)(2,1)}), bf16[64,16,1024]{2,0,1:T(8,128)(2,1)}, u32[]{:S(2)}, u32[]{:S(2)}) %all-to-all-start.3) | async-done | bytes 2097184 | tf_op jit(solution)/shard_map/all_to_all | solution.py:66
  202.8 2.9 %fusion.11 = bf16[64,2,1024]{2,1,0:T(2,128)(2,1)S(1)} fusion(pred[64,2,16]{2,1,0:T(4,128)(4,1)S(1)} %copy.70, bf16[64,16,1024]{2,0,1:T(8,128)(2,1)} %all-to-all-done.3), kind=kOutput, calls=%fused_computation.22 | convolution fusion | flops 4325376 | bytes 2361344 | tf_op jit(solution)/shard_map/rge,red->rgd/dot_general | solution.py:71
  (44 shorter events, 4.7 us)
Async XLA Ops:
  0.6 71.0 %copy-start = (bf16[1,1024,768]{2,1,0:T(8,128)(2,1)S(1)}, bf16[1,1024,768]{2,1,0:T(8,128)(2,1)}, u32[]{:S(2)}) copy-start(bf16[1,1024,768]{2,1,0:T(8,128)(2,1)} %param.10) | copy-start | bytes 4718596
  6.1 7.6 %copy-start.9 = (bf16[128,1024]{1,0:T(8,128)(2,1)S(1)}, bf16[128,1024]{1,0:T(8,128)(2,1)}, u32[]{:S(2)}) copy-start(bf16[128,1024]{1,0:T(8,128)(2,1)} %param.7) | copy-start | bytes 786436
  6.1 56.9 %all-to-all-start.2 = ((bf16[64,16,1024]{2,0,1:T(8,128)(2,1)}), bf16[64,16,1024]{2,0,1:T(8,128)(2,1)}, u32[]{:S(2)}, u32[]{:S(2)}) async-start(bf16[64,16,1024]{2,0,1:T(8,128)(2,1)} %copy.67), calls=%async_computation.2 | async-start | bytes 4194304 | tf_op jit(solution)/shard_map/all_to_all | solution.py:39
  63.0 53.8 %all-to-all-start.1 = ((bf16[64,16,1024]{2,0,1:T(8,128)(2,1)}), bf16[64,16,1024]{2,0,1:T(8,128)(2,1)}, u32[]{:S(2)}, u32[]{:S(2)}) async-start(bf16[64,16,1024]{2,0,1:T(8,128)(2,1)} %copy.64), calls=%async_computation.1 | async-start | bytes 4194304 | tf_op jit(solution)/shard_map/all_to_all | solution.py:40
  70.2 1.4 copy-start.2
  116.8 2.9 %copy-start.1 = (f32[1024,768]{0,1:T(8,128)S(1)}, f32[1024,768]{0,1:T(8,128)}, u32[]{:S(2)}) copy-start(f32[1024,768]{0,1:T(8,128)} %fusion.5) | copy-start | bytes 9437188
  116.8 2.9 %copy-start.11 = (bf16[1,384,1024]{2,1,0:T(8,128)(2,1)S(1)}, bf16[1,384,1024]{2,1,0:T(8,128)(2,1)}, u32[]{:S(2)}) copy-start(bf16[1,384,1024]{2,1,0:T(8,128)(2,1)} %param.11) | copy-start | bytes 2359300
  119.7 2.1 %copy-start.4 = (bf16[64,16,1024]{2,1,0:T(8,128)(2,1)}, bf16[64,16,1024]{2,1,0:T(8,128)(2,1)S(1)}, u32[]{:S(2)}) copy-start(bf16[64,16,1024]{2,1,0:T(8,128)(2,1)S(1)} %copy.65) | copy-start | bytes 6291460
  119.8 6.3 %copy-start.10 = (bf16[128,8]{0,1:T(8,128)(2,1)S(1)}, bf16[128,8]{0,1:T(8,128)(2,1)}, u32[]{:S(2)}) copy-start(bf16[128,8]{0,1:T(8,128)(2,1)} %param.9) | copy-start | bytes 6148
  122.6 9.7 %all-to-all-start.4 = ((bf16[64,16,1]{0,2,1:T(2,128)(2,1)}), bf16[64,16,1]{0,2,1:T(2,128)(2,1)S(1)}, u32[]{:S(2)}, u32[]{:S(2)}) async-start(bf16[64,16,1]{0,2,1:T(2,128)(2,1)} %copy.72), calls=%async_computation.4 | async-start | bytes 16384 | tf_op jit(solution)/shard_map/all_to_all | solution.py:67
  144.4 1.9 copy-start.5
  144.4 1.9 copy-start.7
  148.8 5.3 %copy-start.12 = (bf16[1024,384]{0,1:T(8,128)(2,1)S(1)}, bf16[1024,384]{0,1:T(8,128)(2,1)}, u32[]{:S(2)}) copy-start(bf16[1024,384]{0,1:T(8,128)(2,1)} %get-tuple-element.27) | copy-start | bytes 2359300
  148.8 53.9 %all-to-all-start.3 = ((bf16[64,16,1024]{2,0,1:T(8,128)(2,1)}), bf16[64,16,1024]{2,0,1:T(8,128)(2,1)}, u32[]{:S(2)}, u32[]{:S(2)}) async-start(bf16[64,16,1024]{2,0,1:T(8,128)(2,1)} %copy.69), calls=%async_computation.3 | async-start | bytes 4194304 | tf_op jit(solution)/shard_map/all_to_all | solution.py:66
  154.2 3.7 %copy-start.3 = (bf16[64,16,1024]{2,1,0:T(8,128)(2,1)S(1)}, bf16[64,16,1024]{2,1,0:T(8,128)(2,1)}, u32[]{:S(2)}) copy-start(bf16[64,16,1024]{2,1,0:T(8,128)(2,1)} %copy-done.2) | copy-start | bytes 6291460
  154.2 3.7 %copy-start.6 = (bf16[1024,384]{0,1:T(8,128)(2,1)S(1)}, bf16[1024,384]{0,1:T(8,128)(2,1)}, u32[]{:S(2)}) copy-start(bf16[1024,384]{0,1:T(8,128)(2,1)} %copy-done.5) | copy-start | bytes 2359300
  154.2 3.7 %copy-start.8 = (bf16[1024,384]{0,1:T(8,128)(2,1)S(1)}, bf16[1024,384]{0,1:T(8,128)(2,1)}, u32[]{:S(2)}) copy-start(bf16[1024,384]{0,1:T(8,128)(2,1)} %copy-done.7) | copy-start | bytes 2359300
where the time goes:
time: 207 us; the launch traced here: 206 us
  waiting for transfers between devices  136 us (66%)
  starting transfers between devices  20.1 us (10%)
  local copies, waits for them, and re-layouts  19.5 us (9%)
  matrix products  18.6 us (9%)
  blocking collectives  8.95 us (4%)
  other arithmetic  2.92 us (1%)
    all_to_all x1, waiting for transfers between devices, body(): lax.all_to_all(input_send, ('da', 'db'), split_axis=1, concat_axis=1, til...  45.9 us
    all_to_all x1, waiting for transfers between devices, body(): lax.all_to_all(input_grads, ('da', 'db'), split_axis=1, concat_axis=1, ti...  41.9 us
    all_to_all x1, waiting for transfers between devices, body(): lax.all_to_all(upstream_send, ('da', 'db'), split_axis=1, concat_axis=1,...  41.7 us
    all_to_all x1, blocking collectives, body(): lax.all_to_all(gate_table, ('da', 'db'), split_axis=1, concat_axis=1, til...  8.95 us
    all_to_all x1, starting transfers between devices, body(): lax.all_to_all(input_send, ('da', 'db'), split_axis=1, concat_axis=1, til...  7.57 us
    all_to_all x1, waiting for transfers between devices, body(): lax.all_to_all(score_back, ('da', 'db'), split_axis=1, concat_axis=1, til...  6.08 us
    all_to_all x1, starting transfers between devices, body(): lax.all_to_all(input_grads, ('da', 'db'), split_axis=1, concat_axis=1, ti...  4.57 us
    all_to_all x1, starting transfers between devices, body(): lax.all_to_all(upstream_send, ('da', 'db'), split_axis=1, concat_axis=1,...  4.44 us
  transfers between devices with their start and end apart: 4, of which 4 were waited for; matrix products, arithmetic and copies ran while one was open for 8% of the time, Pallas kernels for 0%

commit v1 on v0

--- a/solution.py
+++ b/solution.py
@@ -62,8 +62,15 @@
     input_grads = jnp.einsum("rf,df->rd", grad_projected, w_in, preferred_element_type=jnp.float32)
     input_grads = input_grads.astype(jnp.bfloat16).reshape(rounds, experts, features)
     score_back = gate_scores.reshape(rounds, experts)
+
+    def turn_floor(point):
+        built = lax.axis_size(("da", "db"))
+        left_arr = jnp.stack(jnp.split(point, built, 1), 0)
+        v_next = lax.all_to_all(left_arr, ("da", "db"), 0, 0)
+        return jnp.concatenate(v_next, 1)
+
     returned, score_ret = (
-        lax.all_to_all(input_grads, ("da", "db"), split_axis=1, concat_axis=1, tiled=True),
+        turn_floor(input_grads),
         lax.all_to_all(score_back, ("da", "db"), split_axis=1, concat_axis=1, tiled=True),
     )
     score_ret = score_ret.reshape(rounds, 1, 1, experts).astype(jnp.float32)

time: 207 us -> 220 us (1.063)
  local copies, waits for them, and re-layouts: 19.5 us -> 32.6 us
    unnamed x28 -> x43, local copies, waits for them, and re-layouts: 2.97 us -> 13.4 us
    split x0 -> x1, local copies, waits for them, and re-layouts: none -> 4.5 us  [turn_floor(): left_arr = jnp.stack(jnp.split(point, built, 1), 0)]
    reshape x1 -> x0, local copies, waits for them, and re-layouts: 2.51 us -> none  [body(): input_grads.astype(jnp.bfloat16).reshape(rounds, experts, features)]
where the time goes in v1:
time: 220 us
  waiting for transfers between devices  136 us (62%)
  local copies, waits for them, and re-layouts  32.6 us (15%)
  starting transfers between devices  20 us (9%)
  matrix products  18.6 us (8%)
  blocking collectives  8.95 us (4%)
  other arithmetic  2.92 us (1%)
    all_to_all x1, waiting for transfers between devices, body(): lax.all_to_all(input_send, ('da', 'db'), split_axis=1, concat_axis=1, til...  45.9 us
    all_to_all x1, waiting for transfers between devices, turn_floor(): v_next = lax.all_to_all(left_arr, ('da', 'db'), 0, 0)  41.9 us
    all_to_all x1, waiting for transfers between devices, body(): lax.all_to_all(upstream_send, ('da', 'db'), split_axis=1, concat_axis=1,...  41.7 us
    unnamed x43, local copies, waits for them, and re-layouts  13.4 us
    all_to_all x1, blocking collectives, body(): lax.all_to_all(gate_table, ('da', 'db'), split_axis=1, concat_axis=1, til...  8.95 us
    all_to_all x1, starting transfers between devices, body(): lax.all_to_all(input_send, ('da', 'db'), split_axis=1, concat_axis=1, til...  7.57 us
    all_to_all x1, waiting for transfers between devices, body(): lax.all_to_all(score_back, ('da', 'db'), split_axis=1, concat_axis=1, til...  6.08 us
    all_to_all x1, starting transfers between devices, turn_floor(): v_next = lax.all_to_all(left_arr, ('da', 'db'), 0, 0)  4.57 us
  transfers between devices with their start and end apart: 4, of which 4 were waited for; matrix products, arithmetic and copies ran while one was open for 8% of the time, Pallas kernels for 0%

profile of v1, /device:TPU:0, one launch (start us, length us, event | category | flops | bytes accessed | tf_op | source)
XLA Modules:
  0.0 219.6 jit_solution(4561392553299459852)
XLA Ops:
  0.6 0.9 copy.149
  1.8 1.1 reshape.94
  3.6 2.5 %copy.160 = bf16[64,16,1024]{2,0,1:T(8,128)(2,1)} copy(bf16[64,16,1024]{2,1,0:T(8,128)(2,1)S(1)} %convolution_convert_fusion) | data formatting | bytes 4194304 | tf_op jit(solution)/shard_map/convert_element_type | solution.py:31
  6.1 7.6 %all-to-all-start.2 = ((bf16[64,16,1024]{2,0,1:T(8,128)(2,1)}), bf16[64,16,1024]{2,0,1:T(8,128)(2,1)}, u32[]{:S(2)}, u32[]{:S(2)}) async-start(bf16[64,16,1024]{2,0,1:T(8,128)(2,1)} %copy.160), calls=%async_computation.2 | async-start | bytes 4194304 | tf_op jit(solution)/shard_map/all_to_all | solution.py:39
  14.6 2.5 %copy.157 = bf16[64,16,1024]{2,0,1:T(8,128)(2,1)} copy(bf16[64,16,1024]{2,1,0:T(8,128)(2,1)S(1)} %convolution_convert_fusion.1) | data formatting | bytes 4194304 | tf_op jit(solution)/shard_map/convert_element_type | solution.py:37
  17.1 45.9 %all-to-all-done.2 = bf16[64,16,1024]{2,0,1:T(8,128)(2,1)} async-done(((bf16[64,16,1024]{2,0,1:T(8,128)(2,1)}), bf16[64,16,1024]{2,0,1:T(8,128)(2,1)}, u32[]{:S(2)}, u32[]{:S(2)}) %all-to-all-start.2) | async-done | bytes 2097184 | tf_op jit(solution)/shard_map/all_to_all | solution.py:39
  63.0 4.4 %all-to-all-start.1 = ((bf16[64,16,1024]{2,0,1:T(8,128)(2,1)}), bf16[64,16,1024]{2,0,1:T(8,128)(2,1)}, u32[]{:S(2)}, u32[]{:S(2)}) async-start(bf16[64,16,1024]{2,0,1:T(8,128)(2,1)} %copy.157), calls=%async_computation.1 | async-start | bytes 4194304 | tf_op jit(solution)/shard_map/all_to_all | solution.py:40
  67.5 2.7 %copy.161 = bf16[64,16,1024]{2,1,0:T(8,128)(2,1)S(1)} copy(bf16[64,16,1024]{2,0,1:T(8,128)(2,1)} %all-to-all-done.2) | data formatting | bytes 4194304 | tf_op jit(solution)/shard_map/all_to_all | solution.py:39
  70.2 1.4 copy-done.2
  71.6 3.5 %fusion.6 = f32[1024,768]{0,1:T(8,128)} fusion(bf16[1024,1024]{1,0:T(8,128)(2,1)S(1)} %bitcast.107, bf16[1,1024,768]{2,1,0:T(8,128)(2,1)S(1)} %copy-done), kind=kOutput, calls=%fused_computation.12 | convolution fusion | flops 1610612736 | bytes 6815744 | tf_op jit(solution)/shard_map/dot_general | solution.py:50
  75.1 41.7 %all-to-all-done.1 = bf16[64,16,1024]{2,0,1:T(8,128)(2,1)} async-done(((bf16[64,16,1024]{2,0,1:T(8,128)(2,1)}), bf16[64,16,1024]{2,0,1:T(8,128)(2,1)}, u32[]{:S(2)}, u32[]{:S(2)}) %all-to-all-start.1) | async-done | bytes 2097184 | tf_op jit(solution)/shard_map/all_to_all | solution.py:40
  116.8 2.9 %copy.158 = bf16[64,16,1024]{2,1,0:T(8,128)(2,1)S(1)} copy(bf16[64,16,1024]{2,0,1:T(8,128)(2,1)} %all-to-all-done.1) | data formatting | bytes 4194304 | tf_op jit(solution)/shard_map/all_to_all | solution.py:40
  119.8 2.1 multiply_reduce_fusion
  122.6 3.5 %all-to-all-start.4 = ((bf16[64,16,1]{0,2,1:T(2,128)(2,1)}), bf16[64,16,1]{0,2,1:T(2,128)(2,1)S(1)}, u32[]{:S(2)}, u32[]{:S(2)}) async-start(bf16[64,16,1]{0,2,1:T(2,128)(2,1)} %copy.180), calls=%async_computation.4 | async-start | bytes 16384 | tf_op jit(solution)/shard_map/all_to_all | solution.py:74
  126.3 6.1 %all-to-all-done.4 = bf16[64,16,1]{0,2,1:T(2,128)(2,1)S(1)} async-done(((bf16[64,16,1]{0,2,1:T(2,128)(2,1)}), bf16[64,16,1]{0,2,1:T(2,128)(2,1)S(1)}, u32[]{:S(2)}, u32[]{:S(2)}) %all-to-all-start.4) | async-done | bytes 2080 | tf_op jit(solution)/shard_map/all_to_all | solution.py:74
  132.4 9.0 %all_to_all.27 = bf16[64,16,1]{0,2,1:T(2,128)(2,1)S(1)} all-to-all(bf16[64,16,1]{0,2,1:T(2,128)(2,1)S(1)} %copy.153), channel_id=1, replica_groups=mesh['groups'=2,'replica'=1,'da'=4,'db'=4] {'da','db'}, dimensions={1} | all-to-all | bytes 4096 | tf_op jit(solution)/shard_map/all_to_all | solution.py:41
  141.6 2.8 %multiply_convert_fusion.4 = (bf16[1024,384]{0,1:T(8,128)(2,1)S(1)}, bf16[1024,384]{0,1:T(8,128)(2,1)S(1)}) fusion(f32[1024,768]{0,1:T(8,128)} %fusion.6, f32[1024,384]{0,1:T(8,128)S(1)} %get-tuple-element.46, f32[1024]{0:T(1024)S(1)} %reshape.101), kind=kLoop, calls=%fused_computation.17 | loop fusion | flops 5505024 | bytes 6295552 | tf_op jit(solution)/shard_map/convert.3
  144.4 1.9 convolution_convert_fusion.2
  146.3 4.5 %fusion.36 = (bf16[64,1,1024]{2,1,0:T(2,128)(2,1)S(1)}, bf16[64,1,1024]{2,1,0:T(2,128)(2,1)S(1)}, bf16[64,1,1024]{2,1,0:T(2,128)(2,1)S(1)}, bf16[64,1,1024]{2,1,...) fusion(bf16[64,16,1024]{2,1,0:T(8,128)(2,1)S(1)} %bitcast.106), kind=kLoop, calls=%fused_computation.66 | loop fusion | bytes 4194304 | tf_op jit(solution)/shard_map/split | solution.py:68
  162.0 4.6 %all-to-all-start.3 = ((bf16[16,64,1,1024]{3,1,2,0:T(8,128)(2,1)}), bf16[16,64,1,1024]{3,1,2,0:T(8,128)(2,1)}, u32[]{:S(2)}, u32[]{:S(2)}) async-start(bf16[16,64,1,1024]{3,1,2,0:T(8,128)(2,1)} %fusion.17), calls=%async_computation.3 | async-start | bytes 4194304 | tf_op jit(solution)/shard_map/all_to_all | solution.py:69
  167.3 3.7 %fusion.11 = bf16[1,384,1024]{2,1,0:T(8,128)(2,1)} fusion(bf16[1024,384]{0,1:T(8,128)(2,1)S(1)} %copy-done.12, bf16[1024,1024]{1,0:T(8,128)(2,1)} %bitcast.110, f32[1024]{0:T(1024)S(1)} %reshape.101), kind=kOutput, calls=%fused_computation.22 | convolution fusion | flops 808845312 | bytes 3674112 | tf_op jit(solution)/shard_map/rf,rd->fd/dot_general | solution.py:98
  171.0 3.0 %fusion.9 = bf16[1,1024,768]{2,1,0:T(8,128)(2,1)} fusion(bf16[1024,1024]{1,0:T(8,128)(2,1)S(1)} %bitcast.108, bf16[1024,384]{0,1:T(8,128)(2,1)S(1)} %copy-done.8, bf16[1024,384]{0,1:T(8,128)(2,1)S(1)} %copy-done.6), kind=kOutput, calls=%fused_computation.20 | convolution fusion | flops 1614544896 | bytes 5242880 | tf_op jit(solution)/shard_map/rd,rf->df/dot_general | solution.py:89
  174.0 41.9 %all-to-all-done.3 = bf16[16,64,1,1024]{3,1,2,0:T(8,128)(2,1)} async-done(((bf16[16,64,1,1024]{3,1,2,0:T(8,128)(2,1)}), bf16[16,64,1,1024]{3,1,2,0:T(8,128)(2,1)}, u32[]{:S(2)}, u32[]{:S(2)}) %all-to-all-start.3) | async-done | bytes 2097184 | tf_op jit(solution)/shard_map/all_to_all | solution.py:69
  215.9 2.9 %fusion.12 = bf16[64,2,1024]{2,1,0:T(2,128)(2,1)S(1)} fusion(pred[64,2,16]{2,1,0:T(4,128)(4,1)S(1)} %copy.179, bf16[16,64,1,1024]{3,1,2,0:T(8,128)(2,1)} %all-to-all-done.3), kind=kOutput, calls=%fused_computation.23 | convolution fusion | flops 4325376 | bytes 2361344 | tf_op jit(solution)/shard_map/rge,red->rgd/dot_general | solution.py:78
  (60 shorter events, 15.9 us)
Async XLA Ops:
  0.6 71.0 %copy-start = (bf16[1,1024,768]{2,1,0:T(8,128)(2,1)S(1)}, bf16[1,1024,768]{2,1,0:T(8,128)(2,1)}, u32[]{:S(2)}) copy-start(bf16[1,1024,768]{2,1,0:T(8,128)(2,1)} %param.10) | copy-start | bytes 4718596
  6.1 7.6 %copy-start.9 = (bf16[128,1024]{1,0:T(8,128)(2,1)S(1)}, bf16[128,1024]{1,0:T(8,128)(2,1)}, u32[]{:S(2)}) copy-start(bf16[128,1024]{1,0:T(8,128)(2,1)} %param.7) | copy-start | bytes 786436
  6.1 56.9 %all-to-all-start.2 = ((bf16[64,16,1024]{2,0,1:T(8,128)(2,1)}), bf16[64,16,1024]{2,0,1:T(8,128)(2,1)}, u32[]{:S(2)}, u32[]{:S(2)}) async-start(bf16[64,16,1024]{2,0,1:T(8,128)(2,1)} %copy.160), calls=%async_computation.2 | async-start | bytes 4194304 | tf_op jit(solution)/shard_map/all_to_all | solution.py:39
  63.0 53.8 %all-to-all-start.1 = ((bf16[64,16,1024]{2,0,1:T(8,128)(2,1)}), bf16[64,16,1024]{2,0,1:T(8,128)(2,1)}, u32[]{:S(2)}, u32[]{:S(2)}) async-start(bf16[64,16,1024]{2,0,1:T(8,128)(2,1)} %copy.157), calls=%async_computation.1 | async-start | bytes 4194304 | tf_op jit(solution)/shard_map/all_to_all | solution.py:40
  70.2 1.4 copy-start.2
  116.8 2.9 %copy-start.1 = (f32[1024,768]{0,1:T(8,128)S(1)}, f32[1024,768]{0,1:T(8,128)}, u32[]{:S(2)}) copy-start(f32[1024,768]{0,1:T(8,128)} %fusion.6) | copy-start | bytes 9437188
  116.8 2.9 %copy-start.11 = (bf16[1,384,1024]{2,1,0:T(8,128)(2,1)S(1)}, bf16[1,384,1024]{2,1,0:T(8,128)(2,1)}, u32[]{:S(2)}) copy-start(bf16[1,384,1024]{2,1,0:T(8,128)(2,1)} %param.11) | copy-start | bytes 2359300
  119.7 2.1 copy-start.4
  119.8 6.3 %copy-start.10 = (bf16[128,8]{0,1:T(8,128)(2,1)S(1)}, bf16[128,8]{0,1:T(8,128)(2,1)}, u32[]{:S(2)}) copy-start(bf16[128,8]{0,1:T(8,128)(2,1)} %param.9) | copy-start | bytes 6148
  122.6 9.7 %all-to-all-start.4 = ((bf16[64,16,1]{0,2,1:T(2,128)(2,1)}), bf16[64,16,1]{0,2,1:T(2,128)(2,1)S(1)}, u32[]{:S(2)}, u32[]{:S(2)}) async-start(bf16[64,16,1]{0,2,1:T(2,128)(2,1)} %copy.180), calls=%async_computation.4 | async-start | bytes 16384 | tf_op jit(solution)/shard_map/all_to_all | solution.py:74
  144.4 1.9 copy-start.5
  144.4 1.9 copy-start.7
  162.0 5.3 %copy-start.12 = (bf16[1024,384]{0,1:T(8,128)(2,1)S(1)}, bf16[1024,384]{0,1:T(8,128)(2,1)}, u32[]{:S(2)}) copy-start(bf16[1024,384]{0,1:T(8,128)(2,1)} %get-tuple-element.27) | copy-start | bytes 2359300
  162.0 53.9 %all-to-all-start.3 = ((bf16[16,64,1,1024]{3,1,2,0:T(8,128)(2,1)}), bf16[16,64,1,1024]{3,1,2,0:T(8,128)(2,1)}, u32[]{:S(2)}, u32[]{:S(2)}) async-start(bf16[16,64,1,1024]{3,1,2,0:T(8,128)(2,1)} %fusion.17), calls=%async_computation.3 | async-start | bytes 4194304 | tf_op jit(solution)/shard_map/all_to_all | solution.py:69
  167.3 3.7 %copy-start.3 = (bf16[64,16,1024]{2,1,0:T(8,128)(2,1)S(1)}, bf16[64,16,1024]{2,1,0:T(8,128)(2,1)}, u32[]{:S(2)}) copy-start(bf16[64,16,1024]{2,1,0:T(8,128)(2,1)} %copy-done.2) | copy-start | bytes 6291460
  167.3 3.7 %copy-start.6 = (bf16[1024,384]{0,1:T(8,128)(2,1)S(1)}, bf16[1024,384]{0,1:T(8,128)(2,1)}, u32[]{:S(2)}) copy-start(bf16[1024,384]{0,1:T(8,128)(2,1)} %copy-done.5) | copy-start | bytes 2359300
  167.3 3.7 %copy-start.8 = (bf16[1024,384]{0,1:T(8,128)(2,1)S(1)}, bf16[1024,384]{0,1:T(8,128)(2,1)}, u32[]{:S(2)}) copy-start(bf16[1024,384]{0,1:T(8,128)(2,1)} %copy-done.7) | copy-start | bytes 2359300
